TPU v7x, 32 devices: a whole 2x2x4 slice. The times are simulated.
32 devices in a mesh: expert: 8 (over z, x), tensor: 4 (over y, core).
Axes of the slice: x: 2, y: 2, z: 4, core: 2. Of those that a mesh axis runs over, the one named last changes fastest.
Arguments:
- tokens: bfloat16 [20480, 1024], P(('expert', 'tensor')), may hold values from -6 to 6
- cotangent: bfloat16 [20480, 1024], P(('expert', 'tensor')), may hold values from -6 to 6
- routes: int32 [20480, 1], P('expert'), may hold values from 0 to 7; in each aligned block of 640 rows (0 to 639, 640 to 1279, ...) at most 112 rows name the same one
- parents: int32 [8, 13], P('expert'), may hold values from 0 to 4, as said below
- ln_attn: float32 [1024], replicated, may hold values from 0.5 to 1.5
- w_qkv: bfloat16 [3, 1024, 1024], P(None, None, 'tensor'), may hold values from -0.1875 to 0.1875
- w_out: bfloat16 [1024, 1024], P('tensor'), may hold values from -3 to 3
- ln_mlp: float32 [1024], replicated, may hold values from 0.5 to 1.5
- w_up: bfloat16 [1024, 4096], P(None, 'tensor'), may hold values from -0.1875 to 0.1875
- w_down: bfloat16 [4096, 1024], P('tensor'), may hold values from -0.09375 to 0.09375
- w_router: bfloat16 [1024, 8], replicated, may hold values from -0.09375 to 0.09375
- w_mix: bfloat16 [1024, 2], replicated, may hold values from -0.1875 to 0.1875
- ex_up: bfloat16 [8, 1024, 4096], P('expert', None, 'tensor'), may hold values from -0.1875 to 0.1875
- ex_down: bfloat16 [8, 4096, 1024], P('expert', 'tensor')
Outputs:
- out: bfloat16 [20480, 1024], P(('expert', 'tensor'))
- grad_tokens: float32 [20480, 1024], P(('expert', 'tensor'))
- grad_ln_attn: float32 [1024], replicated
- grad_qkv: float32 [3, 1024, 1024], P(None, 'expert', 'tensor')
- grad_w_out: float32 [1024, 1024], P('tensor', 'expert')
- grad_ln_mlp: float32 [1024], P('expert')
- grad_up: float32 [1024, 4096], P('expert', 'tensor')
- grad_down: float32 [4096, 1024], P('tensor', 'expert')
- grad_router: float32 [1024, 8], P('expert')
- grad_mix: float32 [1024, 2], P('expert')
- grad_ex_up: float32 [8, 1024, 4096], P('expert', None, 'tensor')
- grad_ex_down: float32 [8, 4096, 1024], P('expert', 'tensor')
Inputs may be any that keep to these rules, and one draw needn't show every extreme that they name: `routes`: in each aligned block of 640 rows (the rows of one device), no expert is named by more than 112 rows, a bound that some block reaches. `parents`: entry j of a row is the parent segment of segment j. Entries 0 to 4 are 0 (the trunk and the four branches hang on the trunk); entries 5 to 12 (the leaves) name each branch 1 to 4 exactly twice.
All inputs are finite; a program needn't handle non-finite values.
Results may differ from a plain program's by a relative error of at most 0.017.
Values may be sent and summed in bfloat16 or wider, within the bound.
No kernel may reach another device: no remote copies, remote signals or barrier semaphores. Data moves between devices by JAX's collectives and lax.ppermute only.
A program may use at most 320 MiB of HBM per device.

v0:
```python
import jax
import jax.numpy as jnp
from jax import lax
from jax.sharding import PartitionSpec as P

HEAD_DIM = 64
TRUNK = 1024
SEG = 128
SEGS = 13
QBLK = 512
TREE_LEN = 2560
EPSILON = 1e-05
NEGATIVE_FILL = -1e30


def norm_parts(values):
    row_mean = jnp.mean(values, axis=-1, keepdims=True)
    centred = values - row_mean
    row_var = jnp.mean(centred * centred, axis=-1, keepdims=True)
    inverse = lax.rsqrt(row_var + EPSILON)
    return (centred * inverse, inverse)


def norm_back(grad_normed, gain_vec, scaled, inverse):
    grad_scaled = grad_normed * gain_vec
    first_mean = jnp.mean(grad_scaled, axis=-1, keepdims=True)
    second = jnp.mean(grad_scaled * scaled, axis=-1, keepdims=True)
    return inverse * (grad_scaled - first_mean - scaled * second)


def gelu_exact(values):
    return jax.nn.gelu(values, approximate=False)


def gelu_slope(values):
    return (
        0.5 * (1.0 + lax.erf(values * 0.7071067811865476))
        + values * jnp.exp(-0.5 * values * values) * 0.3989422804014327
    )


def segment_of(position):
    return jnp.where(position < TRUNK, 0, 1 + (position - TRUNK) // SEG)


def path_mask(parents_row, query_pos, key_pos):
    seg_ids = jnp.arange(SEGS, dtype=jnp.int32)
    query_seg = segment_of(query_pos)
    key_seg = segment_of(key_pos)
    parent_seg = jnp.sum(
        jnp.where(query_seg[:, None] == seg_ids[None, :], parents_row[None, :], 0), axis=1
    )
    grand_seg = jnp.sum(
        jnp.where(parent_seg[:, None] == seg_ids[None, :], parents_row[None, :], 0), axis=1
    )
    on_path = (
        (key_seg[None, :] == query_seg[:, None])
        | (key_seg[None, :] == parent_seg[:, None])
        | (key_seg[None, :] == grand_seg[:, None])
    )
    return on_path & (key_pos[None, :] <= query_pos[:, None])


def block_inputs(qkv_rows, parents, block_index):
    row_start = block_index * QBLK
    tree_index = row_start // TREE_LEN
    queries = lax.dynamic_slice_in_dim(qkv_rows[0], row_start, QBLK, 0).reshape(QBLK, -1, HEAD_DIM)
    key_rows = qkv_rows[1].reshape(TREE_LEN, -1, HEAD_DIM)
    values = qkv_rows[2].reshape(TREE_LEN, -1, HEAD_DIM)
    parents_row = lax.dynamic_index_in_dim(parents, tree_index, 0, keepdims=False)
    raw_scores = jnp.einsum(
        "qhd,khd->hqk", queries, key_rows, preferred_element_type=jnp.float32
    ) * HEAD_DIM ** (-0.5)
    first_row = row_start - tree_index * TREE_LEN
    allowed = path_mask(
        parents_row,
        first_row + jnp.arange(QBLK, dtype=jnp.int32),
        jnp.arange(TREE_LEN, dtype=jnp.int32),
    )
    scores = jnp.where(allowed[None], raw_scores, NEGATIVE_FILL)
    return (row_start, tree_index, queries, key_rows, values, scores)


def to_owners(values, expert_ids, quarter, slot_index, experts, quarters, capacity):
    width = values.shape[1]
    outgoing = jnp.zeros((experts, quarters, capacity, width), jnp.bfloat16)
    outgoing = outgoing.at[expert_ids, quarter, slot_index].set(values)
    return lax.all_to_all(outgoing, "expert", split_axis=0, concat_axis=0, tiled=True)


def to_sources(parts):
    return lax.all_to_all(
        parts.astype(jnp.bfloat16), "expert", split_axis=0, concat_axis=0, tiled=True
    ).astype(parts.dtype)


def per_device(
    tokens,
    cotangent,
    routes,
    parents,
    ln_attn,
    w_qkv,
    w_out,
    ln_mlp,
    w_up,
    w_down,
    w_router,
    w_mix,
    ex_up,
    ex_down,
):
    tok_dev = tokens.shape[0]
    model_width = tokens.shape[1]
    quarters = lax.axis_size("tensor")
    own_start = lax.axis_index("tensor") * tok_dev
    group_rows = tok_dev * quarters
    experts = w_router.shape[1]
    capacity = max(2, tok_dev * 7 // (5 * experts))
    block_total = group_rows // QBLK
    gathered = lax.all_gather(tokens, "tensor", axis=0, tiled=True)
    scaled_one, inverse_one = norm_parts(gathered.astype(jnp.float32))
    normed_one = (scaled_one * ln_attn).astype(jnp.bfloat16)
    qkv_rows = jnp.einsum(
        "td,sdc->stc", normed_one, w_qkv, preferred_element_type=jnp.float32
    ).astype(jnp.bfloat16)

    def attend_block(block_index):
        row_start, tree_index, queries, key_rows, values, scores = block_inputs(
            qkv_rows, parents, block_index
        )
        row_max = jnp.max(scores, axis=-1, keepdims=True)
        weights = jnp.exp(scores - row_max)
        row_total = jnp.sum(weights, axis=-1, keepdims=True)
        weights = (weights / row_total).astype(jnp.bfloat16)
        output = jnp.einsum("hqk,khd->qhd", weights, values, preferred_element_type=jnp.float32)
        return (
            output.reshape(QBLK, -1).astype(jnp.bfloat16),
            (row_max + jnp.log(row_total))[..., 0],
        )

    attended, log_total = lax.map(attend_block, jnp.arange(block_total, dtype=jnp.int32))
    attended = attended.reshape(group_rows, -1)
    residual = tokens.astype(jnp.float32) + lax.psum_scatter(
        jnp.dot(attended, w_out, preferred_element_type=jnp.float32),
        "tensor",
        scatter_dimension=0,
        tiled=True,
    )
    residual_all = lax.all_gather(residual, "tensor", axis=0, tiled=True)
    scaled_two, inverse_two = norm_parts(residual_all)
    normed_two = (scaled_two * ln_mlp).astype(jnp.bfloat16)
    pre_dense = jnp.dot(normed_two, w_up, preferred_element_type=jnp.float32)
    active = gelu_exact(pre_dense).astype(jnp.bfloat16)
    dense_part = jnp.dot(active, w_down, preferred_element_type=jnp.float32)
    router_probs = jax.nn.softmax(
        jnp.dot(normed_two, w_router, preferred_element_type=jnp.float32), axis=-1
    )
    expert_ids = routes[:, 0]
    chosen = expert_ids[:, None] == jnp.arange(experts, dtype=jnp.int32)[None, :]
    gate_prob = jnp.sum(jnp.where(chosen, router_probs, 0.0), axis=1)
    mix_coef = jax.nn.softmax(
        jnp.dot(normed_two, w_mix, preferred_element_type=jnp.float32), axis=-1
    )
    counted = chosen.astype(jnp.int32).reshape(quarters, tok_dev, experts)
    position = (jnp.cumsum(counted, axis=1) - 1).reshape(group_rows, experts)
    slot_index = jnp.sum(jnp.where(chosen, position, 0), axis=1)
    quarter = jnp.arange(group_rows, dtype=jnp.int32) // tok_dev
    arrived = to_owners(normed_two, expert_ids, quarter, slot_index, experts, quarters, capacity)
    flat_rows = arrived.reshape(-1, model_width)
    expert_pre = jnp.dot(flat_rows, ex_up[0], preferred_element_type=jnp.float32)
    expert_active = gelu_exact(expert_pre).astype(jnp.bfloat16)
    expert_part = jnp.dot(expert_active, ex_down[0], preferred_element_type=jnp.float32).reshape(
        arrived.shape
    )
    returned = to_sources(expert_part)
    expert_weight = mix_coef[:, 1] * gate_prob
    expert_rows = returned[expert_ids, quarter, slot_index]
    extra_term = 0.0
    dense_coef = mix_coef[:, 0]
    mixed = (
        lax.psum_scatter(
            (dense_coef[:, None] * dense_part + expert_weight[:, None] * expert_rows).astype(
                jnp.bfloat16
            ),
            "tensor",
            scatter_dimension=0,
            tiled=True,
        ).astype(jnp.float32)
        + extra_term
    )
    out = (residual + mixed).astype(jnp.bfloat16)
    grad_all = lax.all_gather(cotangent, "tensor", axis=0, tiled=True).astype(jnp.float32)
    grad_dense = (mix_coef[:, 0:1] * grad_all).astype(jnp.bfloat16)
    grad_down = jnp.einsum("gf,gd->fd", active, grad_dense, preferred_element_type=jnp.float32)
    grad_active = jnp.einsum("gd,fd->gf", grad_dense, w_down, preferred_element_type=jnp.float32)
    grad_pre = (grad_active * gelu_slope(pre_dense)).astype(jnp.bfloat16)
    grad_up = jnp.einsum("gd,gf->df", normed_two, grad_pre, preferred_element_type=jnp.float32)
    grad_normed_two = jnp.einsum("gf,df->gd", grad_pre, w_up, preferred_element_type=jnp.float32)
    dense_dot = jnp.sum(grad_all * dense_part, axis=1)
    grad_expert = (expert_weight[:, None] * grad_all).astype(jnp.bfloat16)
    arrived_grad = to_owners(
        grad_expert, expert_ids, quarter, slot_index, experts, quarters, capacity
    )
    flat_grad = arrived_grad.reshape(-1, model_width)
    grad_ex_down = jnp.einsum(
        "rf,rd->fd", expert_active, flat_grad, preferred_element_type=jnp.float32
    )[None]
    grad_ex_active = jnp.einsum(
        "rd,fd->rf", flat_grad, ex_down[0], preferred_element_type=jnp.float32
    )
    grad_ex_pre = (grad_ex_active * gelu_slope(expert_pre)).astype(jnp.bfloat16)
    grad_ex_up = jnp.einsum(
        "rd,rf->df", flat_rows, grad_ex_pre, preferred_element_type=jnp.float32
    )[None]
    grad_ex_rows = jnp.einsum(
        "rf,df->rd", grad_ex_pre, ex_up[0], preferred_element_type=jnp.float32
    ).reshape(arrived.shape)
    grad_back = to_sources(grad_ex_rows)
    grad_normed_two = grad_normed_two + grad_back[expert_ids, quarter, slot_index]
    expert_dot = jnp.sum(grad_all * expert_rows, axis=1)
    row_dots = jnp.stack([dense_dot, expert_dot], axis=1)
    grad_normed_two, row_dots = (
        lax.psum(grad_normed_two.astype(jnp.bfloat16), "tensor").astype(jnp.float32),
        lax.psum(row_dots.astype(jnp.bfloat16), "tensor").astype(jnp.float32),
    )
    mix_grad = jnp.stack([row_dots[:, 0], gate_prob * row_dots[:, 1]], axis=1)
    grad_mix_logits = (
        mix_coef * (mix_grad - jnp.sum(mix_coef * mix_grad, axis=1, keepdims=True))
    ).astype(jnp.bfloat16)
    grad_gate = mix_coef[:, 1] * row_dots[:, 1]
    grad_router_logits = (
        router_probs
        * (jnp.where(chosen, grad_gate[:, None], 0.0) - (gate_prob * grad_gate)[:, None])
    ).astype(jnp.bfloat16)
    grad_normed_two = grad_normed_two + jnp.einsum(
        "ge,de->gd", grad_router_logits, w_router, preferred_element_type=jnp.float32
    )
    grad_normed_two = grad_normed_two + jnp.einsum(
        "gm,dm->gd", grad_mix_logits, w_mix, preferred_element_type=jnp.float32
    )
    grad_router = jnp.einsum(
        "gd,ge->de", normed_two, grad_router_logits, preferred_element_type=jnp.float32
    )
    grad_mix = jnp.einsum(
        "gd,gm->dm", normed_two, grad_mix_logits, preferred_element_type=jnp.float32
    )
    grad_ln_mlp = jnp.sum(grad_normed_two * scaled_two, axis=0)
    grad_residual = grad_all + norm_back(grad_normed_two, ln_mlp, scaled_two, inverse_two)
    grad_branch = grad_residual.astype(jnp.bfloat16)
    grad_w_out = jnp.einsum("gc,gd->cd", attended, grad_branch, preferred_element_type=jnp.float32)
    grad_attended = jnp.einsum(
        "gd,cd->gc", grad_branch, w_out, preferred_element_type=jnp.float32
    ).astype(jnp.bfloat16)

    def attend_back(carried, block_index):
        grad_keys, grad_values = carried
        row_start, tree_index, queries, key_rows, values, scores = block_inputs(
            qkv_rows, parents, block_index
        )
        log_block = lax.dynamic_index_in_dim(log_total, block_index, 0, keepdims=False)
        weights = jnp.exp(scores - log_block[..., None])
        grad_block = lax.dynamic_slice_in_dim(grad_attended, row_start, QBLK, 0).reshape(
            QBLK, -1, HEAD_DIM
        )
        grad_weights = jnp.einsum(
            "qhd,khd->hqk", grad_block, values, preferred_element_type=jnp.float32
        )
        inner = jnp.sum(weights * grad_weights, axis=-1, keepdims=True)
        grad_scores = (weights * (grad_weights - inner)).astype(jnp.bfloat16)
        grad_query = jnp.einsum(
            "hqk,khd->qhd", grad_scores, key_rows, preferred_element_type=jnp.float32
        ) * HEAD_DIM ** (-0.5)
        key_part = jnp.einsum(
            "hqk,qhd->khd", grad_scores, queries, preferred_element_type=jnp.float32
        ) * HEAD_DIM ** (-0.5)
        value_part = jnp.einsum(
            "hqk,qhd->khd",
            weights.astype(jnp.bfloat16),
            grad_block,
            preferred_element_type=jnp.float32,
        )
        grad_keys = grad_keys + key_part.reshape(TREE_LEN, -1)
        grad_values = grad_values + value_part.reshape(TREE_LEN, -1)
        return ((grad_keys, grad_values), grad_query.reshape(QBLK, -1).astype(jnp.bfloat16))

    empty_rows = jnp.zeros((group_rows, qkv_rows.shape[2]), jnp.float32)
    (grad_keys, grad_values), grad_queries = lax.scan(
        attend_back, (empty_rows, empty_rows), jnp.arange(block_total, dtype=jnp.int32)
    )
    grad_qkv_rows = jnp.stack(
        [
            grad_queries.reshape(group_rows, -1),
            grad_keys.astype(jnp.bfloat16),
            grad_values.astype(jnp.bfloat16),
        ]
    )
    grad_w_qkv = jnp.einsum(
        "gd,sgc->sdc", normed_one, grad_qkv_rows, preferred_element_type=jnp.float32
    )
    grad_normed_one = jnp.einsum(
        "sgc,sdc->gd", grad_qkv_rows, w_qkv, preferred_element_type=jnp.float32
    )
    part_gain = jnp.sum(grad_normed_one * scaled_one, axis=0)
    grad_normed_own = lax.psum_scatter(
        grad_normed_one.astype(jnp.bfloat16), "tensor", scatter_dimension=0, tiled=True
    ).astype(jnp.float32)
    own_scaled = lax.dynamic_slice_in_dim(scaled_one, own_start, tok_dev, 0)
    own_inverse = lax.dynamic_slice_in_dim(inverse_one, own_start, tok_dev, 0)
    own_residual_grad = lax.dynamic_slice_in_dim(grad_residual, own_start, tok_dev, 0)
    grad_tokens = own_residual_grad + norm_back(grad_normed_own, ln_attn, own_scaled, own_inverse)
    summed_grads = (
        lax.psum_scatter(grad_w_qkv, "expert", scatter_dimension=1, tiled=True),
        lax.psum_scatter(grad_w_out, "expert", scatter_dimension=1, tiled=True),
        lax.psum_scatter(grad_ln_mlp, "expert", scatter_dimension=0, tiled=True),
        lax.psum_scatter(grad_up, "expert", scatter_dimension=0, tiled=True),
        lax.psum_scatter(grad_down, "expert", scatter_dimension=1, tiled=True),
        lax.psum_scatter(grad_router, "expert", scatter_dimension=0, tiled=True),
        lax.psum_scatter(grad_mix, "expert", scatter_dimension=0, tiled=True),
    )
    grad_ln_attn = lax.psum(part_gain, ("expert", "tensor"))
    return (
        out,
        grad_tokens,
        grad_ln_attn,
        summed_grads[0],
        summed_grads[1],
        summed_grads[2],
        summed_grads[3],
        summed_grads[4],
        summed_grads[5],
        summed_grads[6],
        grad_ex_up,
        grad_ex_down,
    )


def solution(mesh):
    return jax.shard_map(
        per_device,
        mesh=mesh,
        in_specs=(
            P(("expert", "tensor"), None),
            P(("expert", "tensor"), None),
            P("expert", None),
            P("expert", None),
            P(),
            P(None, None, "tensor"),
            P("tensor", None),
            P(),
            P(None, "tensor"),
            P("tensor", None),
            P(),
            P(),
            P("expert", None, "tensor"),
            P("expert", "tensor", None),
        ),
        out_specs=(
            P(("expert", "tensor"), None),
            P(("expert", "tensor"), None),
            P(),
            P(None, "expert", "tensor"),
            P("tensor", "expert"),
            P("expert"),
            P("expert", "tensor"),
            P("tensor", "expert"),
            P("expert", None),
            P("expert", None),
            P("expert", None, "tensor"),
            P("expert", "tensor", None),
        ),
        check_vma=False,
    )
```

profile of v0, /device:TPU:0, one launch (start us, length us, event | category | flops | bytes accessed | tf_op | source)
XLA Modules:
  0.0 2363.1 jit_solution(15836324658128825775)
XLA Ops:
  8.0 44.8 %all-gather.4.cloned.1.call-done = bf16[2560,1024]{1,0:T(8,128)(2,1)} async-done(((bf16[640,1024]{1,0:T(8,128)(2,1)}), bf16[2560,1024]{1,0:T(8,128)(2,1)}) %all-gather.4.cloned.1.call-update) | async-done | bytes 5242896 | tf_op jit(solution)/shard_map/all_gather | solution.py:121
  75.0 190.0 %while.33 = (s32[]{:T(128)}, bf16[5,512,256]{2,1,0:T(8,128)(2,1)}, f32[5,4,512]{2,1,0:T(4,128)S(1)}, s32[5]{0:T(128)S(1)}, s32[1,13]{1,0:T(1,128)S(1)}, /*index=...) while((s32[]{:T(128)}, bf16[5,512,256]{2,1,0:T(8,128)(2,1)}, ...), condition=%wide.region_7.8_spmd, body=%wide.region_2.7_spmd.sunk | while | flops 1414493696 | bytes 169976272 | solution.py:142
  100.7 10.5 fusion.210
  138.7 10.5 fusion.210
  176.6 10.5 fusion.210
  214.6 10.5 fusion.210
  252.6 10.5 fusion.210
  272.6 85.0 %reduce-scatter.12.cloned.1.call-done = f32[640,1024]{1,0:T(8,128)} async-done(((f32[2560,1024]{1,0:T(8,128)}), f32[640,1024]{1,0:T(8,128)}) %reduce-scatter.12.cloned.1.call-update) | async-done | bytes 2621456 | tf_op jit(solution)/shard_map/reduce_scatter | solution.py:144
  368.6 63.2 %all-gather.6.cloned.1.call-done = f32[2560,1024]{1,0:T(8,128)} async-done(((f32[640,1024]{1,0:T(8,128)}), f32[2560,1024]{1,0:T(8,128)}) %all-gather.6.cloned.1.call-update) | async-done | bytes 10485776 | tf_op jit(solution)/shard_map/all_gather | solution.py:150
  441.6 18.1 scatter_custom_fusion
  459.7 166.5 %all_to_all.20 = bf16[8,4,112,1024]{3,2,1,0:T(8,128)(2,1)S(1)} all-to-all(bf16[8,4,112,1024]{3,2,1,0:T(8,128)(2,1)} %bitcast.211), channel_id=1, replica_groups=mesh['expert'=8,'tensor'=4] {'expert'}, dimensions={0} | all-to-all | bytes 14680064 | tf_op jit(solution)/shard_map/all_to_all | solution.py:88
  626.2 40.2 %fusion.43 = (bf16[3584,1024]{1,0:T(8,128)(2,1)S(1)}, f32[3584,1024]{1,0:T(8,128)}) fusion(bf16[3584,1024]{1,0:T(8,128)(2,1)S(1)} %bitcast.215, bf16[1,1024,1024]{2,1,0:T(8,128)(2,1)S(1)} %copy-done), kind=kOutput, calls=%fused_computation.106 | convolution fusion | flops 7754743808 | bytes 31457280 | tf_op jit(solution)/shard_map/dot_general | solution.py:171
  669.4 9.9 convolution_convert_fusion.1
  694.0 29.9 %fusion.62 = (bf16[2560,1024]{1,0:T(8,128)(2,1)}, f32[2560,1024]{1,0:T(8,128)}) fusion(bf16[2560,1024]{1,0:T(8,128)(2,1)S(1)} %multiply_convert_fusion.1, bf16[1024,1024]{1,0:T(8,128)(2,1)S(1)} %copy-done.58), kind=kOutput, calls=%fused_computation.135 | convolution fusion | flops 5539102720 | bytes 23068672 | tf_op jit(solution)/shard_map/dot_general | solution.py:153
  723.9 120.1 %all-to-all-done.1 = bf16[8,4,112,1024]{3,2,1,0:T(8,128)(2,1)} async-done(((bf16[8,4,112,1024]{3,2,1,0:T(8,128)(2,1)}), bf16[8,4,112,1024]{3,2,1,0:T(8,128)(2,1)}, u32[]{:S(2)}, u32[]{:S(2)}) %all-to-all-start.1) | async-done | bytes 7340064 | tf_op jit(solution)/shard_map/all_to_all | solution.py:92
  844.1 10.2 convert_element_type.171
  854.2 40.0 %gather_fusion = f32[2560,1024]{1,0:T(8,128)} fusion(f32[8,4,112,1024]{3,2,1,0:T(8,128)} %convert_element_type.171, s32[2560]{0:T(1024)S(1)} %copy-done.3), kind=kCustom, calls=%fused_computation | custom fusion | bytes 21002240 | tf_op jit(solution)/shard_map/gather | solution.py:178
  894.2 15.1 fusion.71
  909.4 10.2 psum.22
  919.9 17.8 scatter_custom_fusion.1
  937.7 164.2 %all_to_all.21 = bf16[8,4,112,1024]{3,2,1,0:T(8,128)(2,1)S(1)} all-to-all(bf16[8,4,112,1024]{3,2,1,0:T(8,128)(2,1)} %bitcast.212), channel_id=1, replica_groups=mesh['expert'=8,'tensor'=4] {'expert'}, dimensions={0} | all-to-all | bytes 14680064 | tf_op jit(solution)/shard_map/all_to_all | solution.py:88
  1101.9 15.5 fusion.49
  1120.4 10.0 convolution_convert_fusion
  1135.5 13.0 fusion.68
  1148.6 146.3 %all-to-all-done.3 = bf16[8,4,112,1024]{3,2,1,0:T(8,128)(2,1)} async-done(((bf16[8,4,112,1024]{3,2,1,0:T(8,128)(2,1)}), bf16[8,4,112,1024]{3,2,1,0:T(8,128)(2,1)}, u32[]{:S(2)}, u32[]{:S(2)}) %all-to-all-start.3) | async-done | bytes 7340064 | tf_op jit(solution)/shard_map/all_to_all | solution.py:92
  1294.9 10.2 convert_element_type.181
  1305.1 40.0 %gather_fusion.1 = f32[2560,1024]{1,0:T(8,128)} fusion(f32[8,4,112,1024]{3,2,1,0:T(8,128)} %convert_element_type.181, s32[2560]{0:T(1024)S(1)} %copy-done.3), kind=kCustom, calls=%fused_computation.1 | custom fusion | bytes 21002240 | tf_op jit(solution)/shard_map/gather | solution.py:220
  1345.1 11.5 add_convert_fusion
  1361.6 10.5 add_convert_fusion.1
  1378.1 79.8 %all-reduce.3.cloned.1.call-done = bf16[2560,1024]{1,0:T(8,128)(2,1)} async-done(((bf16[2560,1024]{1,0:T(8,128)(2,1)}), bf16[2560,1024]{1,0:T(8,128)(2,1)}) %all-reduce.3.cloned.1.call-update) | async-done | bytes 5242896 | tf_op jit(solution)/shard_map/psum | solution.py:224
  1457.9 12.3 multiply_reduce_fusion.1
  1482.8 420.8 %while.34 = (s32[]{:T(128)}, f32[2560,256]{0,1:T(8,128)}, f32[2560,256]{0,1:T(8,128)}, bf16[5,512,256]{2,1,0:T(8,128)(2,1)}, bf16[3,2560,256]{1,2,0:T(8,128)(2,1...) while((s32[]{:T(128)}, f32[2560,256]{0,1:T(8,128)}, ...), condition=%wide.region_33.34_spmd.clone, body=%wide.region_29.33_spmd.clone.sunk | while | flops 3446896640 | bytes 251757168 | solution.py:288
  1493.2 8.6 fusion.222
  1501.8 11.4 fusion.226
  1513.3 15.1 multiply_reduce_fusion.11
  1528.3 22.2 multiply_convert_fusion.9
  1579.1 8.6 fusion.222
  1587.6 11.4 fusion.226
  1599.0 15.1 multiply_reduce_fusion.11
  1614.1 20.0 multiply_convert_fusion.9
  1662.7 8.6 fusion.222
  1671.2 11.4 fusion.226
  1682.6 15.1 multiply_reduce_fusion.11
  1697.7 20.0 multiply_convert_fusion.9
  1746.2 8.6 fusion.222
  1754.8 11.4 fusion.226
  1766.2 15.1 multiply_reduce_fusion.11
  1781.2 20.0 multiply_convert_fusion.9
  1838.4 11.4 fusion.226
  1849.7 15.1 multiply_reduce_fusion.11
  1864.8 20.0 multiply_convert_fusion.9
  1908.5 9.7 convolution_bitcast_fusion.2
  1918.2 11.8 bitcast_convert_fusion
  1934.2 10.7 fusion.93
  1944.9 10.5 fusion.126
  1962.2 13.9 convolution_bitcast_fusion
  1978.7 13.6 convolution_bitcast_fusion.1
  1992.2 21.0 all-reduce
  2013.8 11.6 fusion.73
  2025.4 37.2 %psum.23 = f32[1024]{0:T(1024)} all-reduce(f32[1024]{0:T(1024)S(1)} %get-tuple-element.473), channel_id=1, replica_groups=mesh['expert'=8,'tensor'=4] {'expert','tensor'}, use_global_device_ids=true, to_apply=%region_38.39 | all-reduce | flops 1024 | bytes 8192 | tf_op jit(solution)/shard_map/psum | solution.py:321
  2072.4 32.0 %reduce-scatter.26.cloned.1.call-done = f32[128,8]{0,1:T(8,128)} async-done(((f32[1024,8]{0,1:T(8,128)}), f32[128,8]{0,1:T(8,128)}) %reduce-scatter.26.cloned.1.call-update) | async-done | bytes 4112 | tf_op jit(solution)/shard_map/reduce_scatter | solution.py:318
  2104.4 92.0 %reduce-scatter.24.cloned.1.call-done = f32[1024,128]{1,0:T(8,128)} async-done(((f32[1024,1024]{1,0:T(8,128)}), f32[1024,128]{1,0:T(8,128)}) %reduce-scatter.24.cloned.1.call-update) | async-done | bytes 524304 | tf_op jit(solution)/shard_map/reduce_scatter | solution.py:317
  2196.4 91.9 %reduce-scatter.22.cloned.1.call-done = f32[128,1024]{1,0:T(8,128)} async-done(((f32[1024,1024]{1,0:T(8,128)}), f32[128,1024]{1,0:T(8,128)}) %reduce-scatter.22.cloned.1.call-update) | async-done | bytes 524304 | tf_op jit(solution)/shard_map/reduce_scatter | solution.py:316
  2288.3 68.0 %reduce-scatter.20.cloned.1.call-done = f32[256,128]{1,0:T(8,128)} async-done(((f32[256,1024]{1,0:T(8,128)}), f32[256,128]{1,0:T(8,128)}) %reduce-scatter.20.cloned.1.call-update) | async-done | bytes 131088 | tf_op jit(solution)/shard_map/reduce_scatter | solution.py:314
  (445 shorter events, 399.7 us)
Async XLA Ops:
  7.2 619.0 %copy-start = (bf16[1,1024,1024]{2,1,0:T(8,128)(2,1)S(1)}, bf16[1,1024,1024]{2,1,0:T(8,128)(2,1)}, u32[]{:S(2)}) copy-start(bf16[1,1024,1024]{2,1,0:T(8,128)(2,1)} %param.30) | copy-start | bytes 6291460
  7.2 53.8 %copy-start.49 = (f32[1024]{0:T(1024)S(1)}, f32[1024]{0:T(1024)}, u32[]{:S(2)}) copy-start(f32[1024]{0:T(1024)} %param.22) | copy-start | bytes 12292
  7.2 45.6 %all-gather.4.cloned.1.call-start = ((), (), s32[]{:S(2)}) async-start(), calls=%async_computation.13 | async-start | bytes 6553600 | tf_op jit(solution)/shard_map/all_gather | solution.py:121
  7.9 349.6 %reduce-scatter.12.cloned.1.call-start = ((), (), s32[]{:S(2)}) async-start(), calls=%async_computation.14 | async-start | bytes 13107200 | tf_op jit(solution)/shard_map/reduce_scatter | solution.py:144
  61.0 14.1 copy-start.29
  265.0 92.6 %copy-start.16 = (bf16[640,1024]{1,0:T(8,128)(2,1)S(1)}, bf16[640,1024]{1,0:T(8,128)(2,1)}, u32[]{:S(2)}) copy-start(bf16[640,1024]{1,0:T(8,128)(2,1)} %param.18) | copy-start | bytes 3932164
  272.1 89.4 %copy-start.45 = (s32[2560,1]{0,1:T(1,128)S(1)}, s32[2560,1]{0,1:T(1,128)}, u32[]{:S(2)}) copy-start(s32[2560,1]{0,1:T(1,128)} %param.20) | copy-start | bytes 30724
  272.1 96.3 %copy-start.54 = (s32[3]{0:T(128)S(1)}, s32[3]{0:T(128)}, u32[]{:S(2)}) copy-start(s32[3]{0:T(128)} %constant.392) | copy-start | bytes 40
  272.1 96.4 %copy-start.53 = (s32[3]{0:T(128)S(1)}, s32[3]{0:T(128)}, u32[]{:S(2)}) copy-start(s32[3]{0:T(128)} %constant.395) | copy-start | bytes 40
  272.1 159.7 %all-gather.6.cloned.1.call-start = ((), (), s32[]{:S(2)}) async-start(), calls=%async_computation.15 | async-start | bytes 13107200 | tf_op jit(solution)/shard_map/all_gather | solution.py:150
  361.5 331.9 %copy-start.27 = (s32[2560]{0:T(1024)}, s32[2560]{0:T(1024)S(1)}, u32[]{:S(2)}) copy-start(s32[2560]{0:T(1024)S(1)} %reduce.8) | copy-start | bytes 30724
  368.6 72.9 %copy-start.52 = (s32[2560]{0:T(1024)}, s32[2560]{0:T(1024)S(1)}, u32[]{:S(2)}) copy-start(s32[2560]{0:T(1024)S(1)} %broadcast_select_fusion) | copy-start | bytes 30724
  368.6 72.9 %copy-start.39 = (f32[1024]{0:T(1024)S(1)}, f32[1024]{0:T(1024)}, u32[]{:S(2)}) copy-start(f32[1024]{0:T(1024)} %param.25) | copy-start | bytes 12292
  436.3 248.5 %copy-start.23 = (f32[2560]{0:T(1024)}, f32[2560]{0:T(1024)S(1)}, u32[]{:S(2)}) copy-start(f32[2560]{0:T(1024)S(1)} %broadcast_multiply_fusion.2) | copy-start | bytes 30724
  441.6 243.2 %copy-start.25 = (f32[2560]{0:T(1024)}, f32[2560]{0:T(1024)S(1)}, u32[]{:S(2)}) copy-start(f32[2560]{0:T(1024)S(1)} %add_rsqrt_fusion) | copy-start | bytes 30724
  626.2 40.2 %copy-start.14 = (bf16[8,4,112,1024]{3,2,1,0:T(8,128)(2,1)}, bf16[8,4,112,1024]{3,2,1,0:T(8,128)(2,1)S(1)}, u32[]{:S(2)}) copy-start(bf16[8,4,112,1024]{3,2,1,0:T(8,128)(2,1)S(1)} %all_to_all.20) | copy-start | bytes 22020100
  626.2 43.2 %copy-start.55 = (bf16[1,1024,1024]{2,1,0:T(8,128)(2,1)S(1)}, bf16[1,1024,1024]{2,1,0:T(8,128)(2,1)}, u32[]{:S(2)}) copy-start(bf16[1,1024,1024]{2,1,0:T(8,128)(2,1)} %param.31) | copy-start | bytes 6291460
  679.3 164.8 %all-to-all-start.1 = ((bf16[8,4,112,1024]{3,2,1,0:T(8,128)(2,1)}), bf16[8,4,112,1024]{3,2,1,0:T(8,128)(2,1)}, u32[]{:S(2)}, u32[]{:S(2)}) async-start(bf16[8,4,112,1024]{3,2,1,0:T(8,128)(2,1)} %convolution_convert_fusion.1), calls=%async_computation.2 | async-start | bytes 14680064 | tf_op jit(solution)/shard_map/all_to_all | solution.py:92
  684.2 210.0 %all-gather.8.cloned.1.call-start = ((), (), s32[]{:S(2)}) async-start(), calls=%async_computation.17 | async-start | bytes 6553600 | tf_op jit(solution)/shard_map/all_gather | solution.py:193
  693.3 30.6 %copy-start.31 = (f32[2560]{0:T(1024)}, f32[2560]{0:T(1024)S(1)}, u32[]{:S(2)}) copy-start(f32[2560]{0:T(1024)S(1)} %get-tuple-element.483) | copy-start | bytes 30724
  694.0 29.9 %copy-start.35 = (f32[2560]{0:T(1024)}, f32[2560]{0:T(1024)S(1)}, u32[]{:S(2)}) copy-start(f32[2560]{0:T(1024)S(1)} %fusion.107) | copy-start | bytes 30724
  723.9 130.3 %copy-start.3 = (s32[2560]{0:T(1024)S(1)}, s32[2560]{0:T(1024)}, u32[]{:S(2)}) copy-start(s32[2560]{0:T(1024)} %get-tuple-element.475) | copy-start | bytes 30724
  919.9 441.7 %copy-start.43 = (f32[2560]{0:T(1024)}, f32[2560]{0:T(1024)S(1)}, u32[]{:S(2)}) copy-start(f32[2560]{0:T(1024)S(1)} %get-tuple-element.426) | copy-start | bytes 30724
  937.7 164.2 %copy-start.56 = (bf16[1,1024,1024]{2,1,0:T(8,128)(2,1)S(1)}, bf16[1,1024,1024]{2,1,0:T(8,128)(2,1)}, u32[]{:S(2)}) copy-start(bf16[1,1024,1024]{2,1,0:T(8,128)(2,1)} %param.31) | copy-start | bytes 6291460
  1101.9 15.5 copy-start.15
  1130.4 164.5 %all-to-all-start.3 = ((bf16[8,4,112,1024]{3,2,1,0:T(8,128)(2,1)}), bf16[8,4,112,1024]{3,2,1,0:T(8,128)(2,1)}, u32[]{:S(2)}, u32[]{:S(2)}) async-start(bf16[8,4,112,1024]{3,2,1,0:T(8,128)(2,1)} %convolution_convert_fusion), calls=%async_computation.5 | async-start | bytes 14680064 | tf_op jit(solution)/shard_map/all_to_all | solution.py:92
  1135.5 322.4 %all-reduce.3.cloned.1.call-start = ((), (), s32[]{:S(2)}) async-start(), calls=%async_computation.18 | async-start | bytes 10485760 | tf_op jit(solution)/shard_map/psum | solution.py:224
  1305.1 40.0 %copy-start.59 = (bf16[1024,1024]{1,0:T(8,128)(2,1)S(1)}, bf16[1024,1024]{1,0:T(8,128)(2,1)}, u32[]{:S(2)}) copy-start(bf16[1024,1024]{1,0:T(8,128)(2,1)} %param.26) | copy-start | bytes 6291460
  1356.6 600.3 %reduce-scatter.28.cloned.1.call-start = ((), (), s32[]{:S(2)}) async-start(), calls=%async_computation.25 | async-start | bytes 589824
  1361.6 10.8 copy-start.21
  1361.6 10.8 copy-start.42
  1372.1 85.8 %copy-start.24 = (f32[2560]{0:T(1024)S(1)}, f32[2560]{0:T(1024)}, u32[]{:S(2)}) copy-start(f32[2560]{0:T(1024)} %copy-done.23) | copy-start | bytes 30724
  1372.1 85.8 %copy-start.26 = (f32[2560]{0:T(1024)S(1)}, f32[2560]{0:T(1024)}, u32[]{:S(2)}) copy-start(f32[2560]{0:T(1024)} %copy-done.25) | copy-start | bytes 30724
  1372.1 85.8 %copy-start.40 = (f32[1024]{0:T(1024)S(1)}, f32[1024]{0:T(1024)}, u32[]{:S(2)}) copy-start(f32[1024]{0:T(1024)} %param.25) | copy-start | bytes 12292
  1372.1 85.8 %copy-start.48 = (bf16[1024,2]{0,1:T(2,128)(2,1)S(1)}, bf16[1024,2]{0,1:T(2,128)(2,1)}, u32[]{:S(2)}) copy-start(bf16[1024,2]{0,1:T(2,128)(2,1)} %param.29) | copy-start | bytes 12292
  1372.1 586.2 %reduce-scatter.14.cloned.1.call-start = ((), (), s32[]{:S(2)}) async-start(), calls=%async_computation.16 | async-start | bytes 6553600 | tf_op jit(solution)/shard_map/reduce_scatter | solution.py:182
  1378.0 684.6 %reduce-scatter.18.cloned.1.call-start = ((), (), s32[]{:S(2)}) async-start(), calls=%async_computation.20 | async-start | bytes 3538944 | tf_op jit(solution)/shard_map/reduce_scatter | solution.py:313
  1482.8 425.6 %copy-start.34 = (f32[2560]{0:T(1024)S(1)}, f32[2560]{0:T(1024)}, u32[]{:S(2)}) copy-start(f32[2560]{0:T(1024)} %copy-done.33) | copy-start | bytes 30724
  1482.8 425.6 %copy-start.38 = (f32[2560]{0:T(1024)S(1)}, f32[2560]{0:T(1024)}, u32[]{:S(2)}) copy-start(f32[2560]{0:T(1024)} %copy-done.37) | copy-start | bytes 30724
  1482.8 425.6 %copy-start.50 = (f32[1024]{0:T(1024)S(1)}, f32[1024]{0:T(1024)}, u32[]{:S(2)}) copy-start(f32[1024]{0:T(1024)} %param.22) | copy-start | bytes 12292
  1550.6 13.4 copy-start.6
  1550.6 13.4 copy-start.8
  1634.1 13.4 copy-start.6
  1634.1 13.4 copy-start.8
  1717.7 13.4 copy-start.6
  1717.7 13.4 copy-start.8
  1801.3 13.4 copy-start.6
  1801.3 13.4 copy-start.8
  1884.8 13.4 copy-start.6
  1884.8 13.4 copy-start.8
  1908.4 9.8 copy-start.20
  1918.2 12.0 copy-start.22
  1918.2 146.4 %reduce-scatter.16.cloned.1.call-start = ((), (), s32[]{:S(2)}) async-start(), calls=%async_computation.19 | async-start | bytes 6553600 | tf_op jit(solution)/shard_map/reduce_scatter | solution.py:305
  1930.1 174.3 %reduce-scatter.26.cloned.1.call-start = ((), (), s32[]{:S(2)}) async-start(), calls=%async_computation.24 | async-start | bytes 36864 | tf_op jit(solution)/shard_map/reduce_scatter | solution.py:318
  1934.1 262.3 %reduce-scatter.24.cloned.1.call-start = ((), (), s32[]{:S(2)}) async-start(), calls=%async_computation.23 | async-start | bytes 4718592 | tf_op jit(solution)/shard_map/reduce_scatter | solution.py:317
  1944.9 10.7 copy-start.63
  1944.9 343.4 %reduce-scatter.22.cloned.1.call-start = ((), (), s32[]{:S(2)}) async-start(), calls=%async_computation.22 | async-start | bytes 4718592 | tf_op jit(solution)/shard_map/reduce_scatter | solution.py:316
  1955.5 400.8 %reduce-scatter.20.cloned.1.call-start = ((), (), s32[]{:S(2)}) async-start(), calls=%async_computation.21 | async-start | bytes 1179648 | tf_op jit(solution)/shard_map/reduce_scatter | solution.py:314
  1958.4 17.8 slice-start
  1962.2 13.9 slice-start.1
  1962.2 13.9 slice-start.2
  1962.2 14.0 copy-start.13
  1978.7 13.6 copy-start.51
  2013.8 342.5 %copy-start.1 = (bf16[1,1024,1024]{2,1,0:T(8,128)(2,1)S(1)}, bf16[1,1024,1024]{2,1,0:T(8,128)(2,1)}, u32[]{:S(2)}) copy-start(bf16[1,1024,1024]{2,1,0:T(8,128)(2,1)} %param.30) | copy-start | bytes 6291460
  (46 other events, 210.8 us)
Sparse Core Ops, SparseCore 0:
  9.6 43.1 all-gather.3
  272.2 85.2 reduce-scatter.11
  361.6 70.1 all-gather.5
  686.3 40.8 all-gather.7
  1356.7 101.0 all-reduce.2
  1461.1 62.0 reduce-scatter.27
  1525.9 50.3 reduce-scatter.13
  1918.3 74.8 reduce-scatter.17
  1995.7 51.2 reduce-scatter.15
  2050.8 53.5 reduce-scatter.25
  2109.0 87.2 reduce-scatter.23
  2200.4 87.8 reduce-scatter.21
  2292.6 63.6 reduce-scatter.19
where the time goes:
time: 2370 us; the launch traced here: 2360 us
  waiting for transfers between devices  825 us (35%)
  matrix products  585 us (25%)
  blocking collectives  399 us (17%)
  other arithmetic  293 us (12%)
  local copies, waits for them, and re-layouts  217 us (9%)
    all_to_all x2, blocking collectives, to_owners(): lax.all_to_all(outgoing, 'expert', split_axis=0, concat_axis=0, tiled=True)  331 us
    all_to_all x2, waiting for transfers between devices, to_sources(): lax.all_to_all(parts.astype(jnp.bfloat16), 'expert', split_axis=0, concat...  266 us
    convert_element_type x5, other arithmetic, attend_back(): grad_scores = (weights * (grad_weights - inner)).astype(jnp.bfloat16)  102 us
    reduce_scatter x1, waiting for transfers between devices, per_device(): lax.psum_scatter(grad_down, 'expert', scatter_dimension=1, tiled=True)  92 us
    reduce_scatter x1, waiting for transfers between devices, per_device(): lax.psum_scatter(grad_up, 'expert', scatter_dimension=0, tiled=True)  91.9 us
    reduce_scatter x1, waiting for transfers between devices, per_device(): lax.psum_scatter(jnp.dot(attended, w_out, preferred_element_type=jnp.floa...  85 us
    psum x1, waiting for transfers between devices, per_device(): lax.psum(grad_normed_two.astype(jnp.bfloat16), 'tensor').astype(jnp.float32)  79.8 us
    dot_general x5, matrix products, attend_back(): jnp.einsum('qhd,khd->hqk', grad_block, values, preferred_element_type=jnp...  75.3 us
  transfers between devices with their start and end apart: 15, of which 10 were waited for; matrix products, arithmetic and copies ran while one was open for 28% of the time, Pallas kernels for 0%

commit v1 on v0

--- a/solution.py
+++ b/solution.py
@@ -11,6 +11,12 @@
 TREE_LEN = 2560
 EPSILON = 1e-05
 NEGATIVE_FILL = -1e30
+
+
+def add_all(x, axis):
+    shards = lax.all_gather(x, axis, axis=0, tiled=False)
+    result = shards.sum(axis=0)
+    return result
 
 
 def norm_parts(values):
@@ -221,7 +227,7 @@
     expert_dot = jnp.sum(grad_all * expert_rows, axis=1)
     row_dots = jnp.stack([dense_dot, expert_dot], axis=1)
     grad_normed_two, row_dots = (
-        lax.psum(grad_normed_two.astype(jnp.bfloat16), "tensor").astype(jnp.float32),
+        add_all(grad_normed_two.astype(jnp.bfloat16), "tensor").astype(jnp.float32),
         lax.psum(row_dots.astype(jnp.bfloat16), "tensor").astype(jnp.float32),
     )
     mix_grad = jnp.stack([row_dots[:, 0], gate_prob * row_dots[:, 1]], axis=1)

time: 2370 us -> 2410 us (1.017)
  waiting for transfers between devices: 825 us -> 850 us
    all_gather x0 -> x1, waiting for transfers between devices: none -> 106 us  [add_all(): shards = lax.all_gather(x, axis, axis=0, tiled=False)]
    psum x1 -> x0, waiting for transfers between devices: 79.8 us -> none  [per_device(): lax.psum(grad_normed_two.astype(jnp.bfloat16), 'tensor').astype(jnp.float32)]
where the time goes in v1:
time: 2410 us
  waiting for transfers between devices  850 us (35%)
  matrix products  586 us (24%)
  blocking collectives  400 us (17%)
  other arithmetic  309 us (13%)
  local copies, waits for them, and re-layouts  217 us (9%)
    all_to_all x2, blocking collectives, to_owners(): lax.all_to_all(outgoing, 'expert', split_axis=0, concat_axis=0, tiled=True)  331 us
    all_to_all x2, waiting for transfers between devices, to_sources(): lax.all_to_all(parts.astype(jnp.bfloat16), 'expert', split_axis=0, concat...  267 us
    all_gather x1, waiting for transfers between devices, add_all(): shards = lax.all_gather(x, axis, axis=0, tiled=False)  106 us
    convert_element_type x5, other arithmetic, attend_back(): grad_scores = (weights * (grad_weights - inner)).astype(jnp.bfloat16)  101 us
    reduce_scatter x1, waiting for transfers between devices, per_device(): lax.psum_scatter(grad_down, 'expert', scatter_dimension=1, tiled=True)  92 us
    reduce_scatter x1, waiting for transfers between devices, per_device(): lax.psum_scatter(grad_up, 'expert', scatter_dimension=0, tiled=True)  91.8 us
    reduce_scatter x1, waiting for transfers between devices, per_device(): lax.psum_scatter(jnp.dot(attended, w_out, preferred_element_type=jnp.floa...  85 us
    dot_general x5, matrix products, attend_back(): jnp.einsum('qhd,khd->hqk', grad_block, values, preferred_element_type=jnp...  77.1 us
  transfers between devices with their start and end apart: 15, of which 10 were waited for; matrix products, arithmetic and copies ran while one was open for 28% of the time, Pallas kernels for 0%

profile of v1, /device:TPU:0, one launch (start us, length us, event | category | flops | bytes accessed | tf_op | source)
XLA Modules:
  0.0 2407.0 jit_solution(15231439711430115044)
XLA Ops:
  8.0 44.8 %all-gather.6.cloned.1.call-done = bf16[2560,1024]{1,0:T(8,128)(2,1)} async-done(((bf16[640,1024]{1,0:T(8,128)(2,1)}), bf16[2560,1024]{1,0:T(8,128)(2,1)}) %all-gather.6.cloned.1.call-update) | async-done | bytes 5242896 | tf_op jit(solution)/shard_map/all_gather | solution.py:127
  75.1 189.9 %while.33 = (s32[]{:T(128)}, bf16[5,512,256]{2,1,0:T(8,128)(2,1)}, f32[5,4,512]{2,1,0:T(4,128)S(1)}, s32[5]{0:T(128)S(1)}, s32[1,13]{1,0:T(1,128)S(1)}, /*index=...) while((s32[]{:T(128)}, bf16[5,512,256]{2,1,0:T(8,128)(2,1)}, ...), condition=%wide.region_7.8_spmd, body=%wide.region_2.7_spmd.sunk | while | flops 1414493696 | bytes 169976272 | solution.py:148
  100.7 10.5 fusion.210
  138.7 10.5 fusion.210
  176.7 10.5 fusion.210
  214.6 10.5 fusion.210
  252.6 10.5 fusion.210
  272.6 85.0 %reduce-scatter.12.cloned.1.call-done = f32[640,1024]{1,0:T(8,128)} async-done(((f32[2560,1024]{1,0:T(8,128)}), f32[640,1024]{1,0:T(8,128)}) %reduce-scatter.12.cloned.1.call-update) | async-done | bytes 2621456 | tf_op jit(solution)/shard_map/reduce_scatter | solution.py:150
  368.6 63.2 %all-gather.8.cloned.1.call-done = f32[2560,1024]{1,0:T(8,128)} async-done(((f32[640,1024]{1,0:T(8,128)}), f32[2560,1024]{1,0:T(8,128)}) %all-gather.8.cloned.1.call-update) | async-done | bytes 10485776 | tf_op jit(solution)/shard_map/all_gather | solution.py:156
  441.6 18.1 scatter_custom_fusion
  459.7 166.5 %all_to_all.20 = bf16[8,4,112,1024]{3,2,1,0:T(8,128)(2,1)S(1)} all-to-all(bf16[8,4,112,1024]{3,2,1,0:T(8,128)(2,1)} %bitcast.212), channel_id=1, replica_groups=mesh['expert'=8,'tensor'=4] {'expert'}, dimensions={0} | all-to-all | bytes 14680064 | tf_op jit(solution)/shard_map/all_to_all | solution.py:94
  626.2 40.2 %fusion.43 = (bf16[3584,1024]{1,0:T(8,128)(2,1)S(1)}, f32[3584,1024]{1,0:T(8,128)}) fusion(bf16[3584,1024]{1,0:T(8,128)(2,1)S(1)} %bitcast.219, bf16[1,1024,1024]{2,1,0:T(8,128)(2,1)S(1)} %copy-done), kind=kOutput, calls=%fused_computation.106 | convolution fusion | flops 7754743808 | bytes 31457280 | tf_op jit(solution)/shard_map/dot_general | solution.py:177
  669.4 10.0 convolution_convert_fusion.1
  694.2 29.9 %fusion.62 = (bf16[2560,1024]{1,0:T(8,128)(2,1)}, f32[2560,1024]{1,0:T(8,128)}) fusion(bf16[2560,1024]{1,0:T(8,128)(2,1)S(1)} %multiply_convert_fusion.1, bf16[1024,1024]{1,0:T(8,128)(2,1)S(1)} %copy-done.64), kind=kOutput, calls=%fused_computation.135 | convolution fusion | flops 5539102720 | bytes 23068672 | tf_op jit(solution)/shard_map/dot_general | solution.py:159
  724.1 120.1 %all-to-all-done.1 = bf16[8,4,112,1024]{3,2,1,0:T(8,128)(2,1)} async-done(((bf16[8,4,112,1024]{3,2,1,0:T(8,128)(2,1)}), bf16[8,4,112,1024]{3,2,1,0:T(8,128)(2,1)}, u32[]{:S(2)}, u32[]{:S(2)}) %all-to-all-start.1) | async-done | bytes 7340064 | tf_op jit(solution)/shard_map/all_to_all | solution.py:98
  844.2 10.2 convert_element_type.173
  854.4 40.0 %gather_fusion = f32[2560,1024]{1,0:T(8,128)} fusion(f32[8,4,112,1024]{3,2,1,0:T(8,128)} %convert_element_type.173, s32[2560]{0:T(1024)S(1)} %copy-done.3), kind=kCustom, calls=%fused_computation | custom fusion | bytes 21002240 | tf_op jit(solution)/shard_map/gather | solution.py:184
  894.3 15.1 fusion.71
  909.6 10.2 psum.14
  920.1 17.7 scatter_custom_fusion.1
  937.7 164.2 %all_to_all.21 = bf16[8,4,112,1024]{3,2,1,0:T(8,128)(2,1)S(1)} all-to-all(bf16[8,4,112,1024]{3,2,1,0:T(8,128)(2,1)} %bitcast.213), channel_id=1, replica_groups=mesh['expert'=8,'tensor'=4] {'expert'}, dimensions={0} | all-to-all | bytes 14680064 | tf_op jit(solution)/shard_map/all_to_all | solution.py:94
  1101.9 15.5 fusion.49
  1120.4 10.0 convolution_convert_fusion
  1135.4 13.0 fusion.68
  1148.4 146.4 %all-to-all-done.3 = bf16[8,4,112,1024]{3,2,1,0:T(8,128)(2,1)} async-done(((bf16[8,4,112,1024]{3,2,1,0:T(8,128)(2,1)}), bf16[8,4,112,1024]{3,2,1,0:T(8,128)(2,1)}, u32[]{:S(2)}, u32[]{:S(2)}) %all-to-all-start.3) | async-done | bytes 7340064 | tf_op jit(solution)/shard_map/all_to_all | solution.py:98
  1294.8 10.2 convert_element_type.183
  1305.0 40.0 %gather_fusion.1 = f32[2560,1024]{1,0:T(8,128)} fusion(f32[8,4,112,1024]{3,2,1,0:T(8,128)} %convert_element_type.183, s32[2560]{0:T(1024)S(1)} %copy-done.3), kind=kCustom, calls=%fused_computation.1 | custom fusion | bytes 21002240 | tf_op jit(solution)/shard_map/gather | solution.py:226
  1345.0 11.4 add_convert_fusion
  1361.6 13.9 add_convert_fusion.1
  1381.3 105.6 %all-gather.12.cloned.1.call-done = bf16[10240,1024]{1,0:T(8,128)(2,1)} async-done(((bf16[2560,1024]{1,0:T(8,128)(2,1)}), bf16[10240,1024]{1,0:T(8,128)(2,1)}) %all-gather.12.cloned.1.call-update) | async-done | bytes 20971536 | tf_op jit(solution)/shard_map/all_gather | solution.py:17
  1486.9 14.9 reduce_sum.257
  1501.9 12.5 multiply_reduce_fusion.1
  1526.0 420.9 %while.34 = (s32[]{:T(128)}, f32[2560,256]{0,1:T(8,128)}, f32[2560,256]{0,1:T(8,128)}, bf16[5,512,256]{2,1,0:T(8,128)(2,1)}, bf16[3,2560,256]{1,2,0:T(8,128)(2,1...) while((s32[]{:T(128)}, f32[2560,256]{0,1:T(8,128)}, ...), condition=%wide.region_33.34_spmd.clone, body=%wide.region_29.33_spmd.clone.sunk | while | flops 3446896640 | bytes 251757168 | solution.py:294
  1536.4 8.6 fusion.222
  1544.9 11.4 fusion.226
  1556.4 16.8 multiply_reduce_fusion.11
  1573.2 20.6 multiply_convert_fusion.9
  1630.9 11.3 fusion.226
  1642.3 15.1 multiply_reduce_fusion.11
  1657.3 20.0 multiply_convert_fusion.9
  1705.9 8.6 fusion.222
  1714.5 11.4 fusion.226
  1725.9 15.1 multiply_reduce_fusion.11
  1740.9 20.0 multiply_convert_fusion.9
  1789.5 8.6 fusion.222
  1798.1 11.4 fusion.226
  1809.4 15.1 multiply_reduce_fusion.11
  1824.5 20.0 multiply_convert_fusion.9
  1881.6 11.4 fusion.226
  1893.0 15.1 multiply_reduce_fusion.11
  1908.1 20.0 multiply_convert_fusion.9
  1951.7 9.7 convolution_bitcast_fusion.2
  1961.5 11.8 bitcast_convert_fusion
  1977.4 10.7 fusion.93
  1988.2 10.6 fusion.126
  2005.5 14.0 convolution_bitcast_fusion
  2022.1 13.5 convolution_bitcast_fusion.1
  2035.6 21.6 all-reduce
  2057.8 11.7 fusion.73
  2069.5 37.1 %psum.15 = f32[1024]{0:T(1024)} all-reduce(f32[1024]{0:T(1024)S(1)} %get-tuple-element.473), channel_id=1, replica_groups=mesh['expert'=8,'tensor'=4] {'expert','tensor'}, use_global_device_ids=true, to_apply=%region_38.39 | all-reduce | flops 1024 | bytes 8192 | tf_op jit(solution)/shard_map/psum | solution.py:327
  2116.4 32.1 %reduce-scatter.26.cloned.1.call-done = f32[128,8]{0,1:T(8,128)} async-done(((f32[1024,8]{0,1:T(8,128)}), f32[128,8]{0,1:T(8,128)}) %reduce-scatter.26.cloned.1.call-update) | async-done | bytes 4112 | tf_op jit(solution)/shard_map/reduce_scatter | solution.py:324
  2148.5 92.0 %reduce-scatter.24.cloned.1.call-done = f32[1024,128]{1,0:T(8,128)} async-done(((f32[1024,1024]{1,0:T(8,128)}), f32[1024,128]{1,0:T(8,128)}) %reduce-scatter.24.cloned.1.call-update) | async-done | bytes 524304 | tf_op jit(solution)/shard_map/reduce_scatter | solution.py:323
  2240.5 91.8 %reduce-scatter.22.cloned.1.call-done = f32[128,1024]{1,0:T(8,128)} async-done(((f32[1024,1024]{1,0:T(8,128)}), f32[128,1024]{1,0:T(8,128)}) %reduce-scatter.22.cloned.1.call-update) | async-done | bytes 524304 | tf_op jit(solution)/shard_map/reduce_scatter | solution.py:322
  2332.3 68.0 %reduce-scatter.20.cloned.1.call-done = f32[256,128]{1,0:T(8,128)} async-done(((f32[256,1024]{1,0:T(8,128)}), f32[256,128]{1,0:T(8,128)}) %reduce-scatter.20.cloned.1.call-update) | async-done | bytes 131088 | tf_op jit(solution)/shard_map/reduce_scatter | solution.py:320
  (463 shorter events, 407.2 us)
Async XLA Ops:
  7.2 619.0 %copy-start = (bf16[1,1024,1024]{2,1,0:T(8,128)(2,1)S(1)}, bf16[1,1024,1024]{2,1,0:T(8,128)(2,1)}, u32[]{:S(2)}) copy-start(bf16[1,1024,1024]{2,1,0:T(8,128)(2,1)} %param.30) | copy-start | bytes 6291460
  7.2 53.8 %copy-start.55 = (f32[1024]{0:T(1024)S(1)}, f32[1024]{0:T(1024)}, u32[]{:S(2)}) copy-start(f32[1024]{0:T(1024)} %param.22) | copy-start | bytes 12292
  7.2 45.6 %all-gather.6.cloned.1.call-start = ((), (), s32[]{:S(2)}) async-start(), calls=%async_computation.13 | async-start | bytes 6553600 | tf_op jit(solution)/shard_map/all_gather | solution.py:127
  7.9 349.6 %reduce-scatter.12.cloned.1.call-start = ((), (), s32[]{:S(2)}) async-start(), calls=%async_computation.14 | async-start | bytes 13107200 | tf_op jit(solution)/shard_map/reduce_scatter | solution.py:150
  61.0 14.1 copy-start.29
  265.0 92.6 %copy-start.16 = (bf16[640,1024]{1,0:T(8,128)(2,1)S(1)}, bf16[640,1024]{1,0:T(8,128)(2,1)}, u32[]{:S(2)}) copy-start(bf16[640,1024]{1,0:T(8,128)(2,1)} %param.18) | copy-start | bytes 3932164
  272.1 89.4 %copy-start.51 = (s32[2560,1]{0,1:T(1,128)S(1)}, s32[2560,1]{0,1:T(1,128)}, u32[]{:S(2)}) copy-start(s32[2560,1]{0,1:T(1,128)} %param.20) | copy-start | bytes 30724
  272.1 96.3 %copy-start.60 = (s32[3]{0:T(128)S(1)}, s32[3]{0:T(128)}, u32[]{:S(2)}) copy-start(s32[3]{0:T(128)} %constant.393) | copy-start | bytes 40
  272.1 96.4 %copy-start.59 = (s32[3]{0:T(128)S(1)}, s32[3]{0:T(128)}, u32[]{:S(2)}) copy-start(s32[3]{0:T(128)} %constant.396) | copy-start | bytes 40
  272.1 159.7 %all-gather.8.cloned.1.call-start = ((), (), s32[]{:S(2)}) async-start(), calls=%async_computation.15 | async-start | bytes 13107200 | tf_op jit(solution)/shard_map/all_gather | solution.py:156
  361.5 332.0 %copy-start.27 = (s32[2560]{0:T(1024)}, s32[2560]{0:T(1024)S(1)}, u32[]{:S(2)}) copy-start(s32[2560]{0:T(1024)S(1)} %reduce.9) | copy-start | bytes 30724
  368.6 72.9 %copy-start.58 = (s32[2560]{0:T(1024)}, s32[2560]{0:T(1024)S(1)}, u32[]{:S(2)}) copy-start(s32[2560]{0:T(1024)S(1)} %broadcast_select_fusion) | copy-start | bytes 30724
  368.6 72.9 %copy-start.43 = (f32[1024]{0:T(1024)S(1)}, f32[1024]{0:T(1024)}, u32[]{:S(2)}) copy-start(f32[1024]{0:T(1024)} %param.25) | copy-start | bytes 12292
  436.3 248.6 %copy-start.23 = (f32[2560]{0:T(1024)}, f32[2560]{0:T(1024)S(1)}, u32[]{:S(2)}) copy-start(f32[2560]{0:T(1024)S(1)} %broadcast_multiply_fusion.2) | copy-start | bytes 30724
  441.6 243.4 %copy-start.25 = (f32[2560]{0:T(1024)}, f32[2560]{0:T(1024)S(1)}, u32[]{:S(2)}) copy-start(f32[2560]{0:T(1024)S(1)} %add_rsqrt_fusion) | copy-start | bytes 30724
  626.2 40.2 %copy-start.14 = (bf16[8,4,112,1024]{3,2,1,0:T(8,128)(2,1)}, bf16[8,4,112,1024]{3,2,1,0:T(8,128)(2,1)S(1)}, u32[]{:S(2)}) copy-start(bf16[8,4,112,1024]{3,2,1,0:T(8,128)(2,1)S(1)} %all_to_all.20) | copy-start | bytes 22020100
  626.2 43.3 %copy-start.61 = (bf16[1,1024,1024]{2,1,0:T(8,128)(2,1)S(1)}, bf16[1,1024,1024]{2,1,0:T(8,128)(2,1)}, u32[]{:S(2)}) copy-start(bf16[1,1024,1024]{2,1,0:T(8,128)(2,1)} %param.31) | copy-start | bytes 6291460
  679.4 164.8 %all-to-all-start.1 = ((bf16[8,4,112,1024]{3,2,1,0:T(8,128)(2,1)}), bf16[8,4,112,1024]{3,2,1,0:T(8,128)(2,1)}, u32[]{:S(2)}, u32[]{:S(2)}) async-start(bf16[8,4,112,1024]{3,2,1,0:T(8,128)(2,1)} %convolution_convert_fusion.1), calls=%async_computation.2 | async-start | bytes 14680064 | tf_op jit(solution)/shard_map/all_to_all | solution.py:98
  684.3 210.0 %all-gather.10.cloned.1.call-start = ((), (), s32[]{:S(2)}) async-start(), calls=%async_computation.17 | async-start | bytes 6553600 | tf_op jit(solution)/shard_map/all_gather | solution.py:199
  693.5 30.6 %copy-start.31 = (f32[2560]{0:T(1024)}, f32[2560]{0:T(1024)S(1)}, u32[]{:S(2)}) copy-start(f32[2560]{0:T(1024)S(1)} %get-tuple-element.483) | copy-start | bytes 30724
  694.1 30.0 %copy-start.37 = (f32[2560]{0:T(1024)}, f32[2560]{0:T(1024)S(1)}, u32[]{:S(2)}) copy-start(f32[2560]{0:T(1024)S(1)} %fusion.107) | copy-start | bytes 30724
  724.1 130.3 %copy-start.3 = (s32[2560]{0:T(1024)S(1)}, s32[2560]{0:T(1024)}, u32[]{:S(2)}) copy-start(s32[2560]{0:T(1024)} %get-tuple-element.475) | copy-start | bytes 30724
  919.8 436.8 %copy-start.39 = (f32[2560,1]{0,1:T(1,128)}, f32[2560,1]{0,1:T(1,128)S(1)}, u32[]{:S(2)}) copy-start(f32[2560,1]{0,1:T(1,128)S(1)} %reshape_multiply_fusion) | copy-start | bytes 30724
  919.9 436.7 %copy-start.33 = (f32[2560,2]{0,1:T(2,128)}, f32[2560,2]{0,1:T(2,128)S(1)}, u32[]{:S(2)}) copy-start(f32[2560,2]{0,1:T(2,128)S(1)} %get-tuple-element.458) | copy-start | bytes 61444
  919.9 436.7 %copy-start.47 = (f32[2560]{0:T(1024)}, f32[2560]{0:T(1024)S(1)}, u32[]{:S(2)}) copy-start(f32[2560]{0:T(1024)S(1)} %get-tuple-element.457) | copy-start | bytes 30724
  920.0 441.5 %copy-start.49 = (f32[2560]{0:T(1024)}, f32[2560]{0:T(1024)S(1)}, u32[]{:S(2)}) copy-start(f32[2560]{0:T(1024)S(1)} %get-tuple-element.426) | copy-start | bytes 30724
  937.7 164.2 %copy-start.62 = (bf16[1,1024,1024]{2,1,0:T(8,128)(2,1)S(1)}, bf16[1,1024,1024]{2,1,0:T(8,128)(2,1)}, u32[]{:S(2)}) copy-start(bf16[1,1024,1024]{2,1,0:T(8,128)(2,1)} %param.31) | copy-start | bytes 6291460
  1101.9 15.5 copy-start.15
  1130.4 164.4 %all-to-all-start.3 = ((bf16[8,4,112,1024]{3,2,1,0:T(8,128)(2,1)}), bf16[8,4,112,1024]{3,2,1,0:T(8,128)(2,1)}, u32[]{:S(2)}, u32[]{:S(2)}) async-start(bf16[8,4,112,1024]{3,2,1,0:T(8,128)(2,1)} %convolution_convert_fusion), calls=%async_computation.5 | async-start | bytes 14680064 | tf_op jit(solution)/shard_map/all_to_all | solution.py:98
  1135.4 351.5 %all-gather.12.cloned.1.call-start = ((), (), s32[]{:S(2)}) async-start(), calls=%async_computation.24 | async-start | bytes 26214400 | tf_op jit(solution)/shard_map/all_gather | solution.py:17
  1305.0 40.1 %copy-start.65 = (bf16[1024,1024]{1,0:T(8,128)(2,1)S(1)}, bf16[1024,1024]{1,0:T(8,128)(2,1)}, u32[]{:S(2)}) copy-start(bf16[1024,1024]{1,0:T(8,128)(2,1)} %param.26) | copy-start | bytes 6291460
  1356.5 643.7 %reduce-scatter.28.cloned.1.call-start = ((), (), s32[]{:S(2)}) async-start(), calls=%async_computation.25 | async-start | bytes 589824
  1361.5 14.3 copy-start.21
  1361.6 14.3 copy-start.46
  1375.5 626.1 %reduce-scatter.14.cloned.1.call-start = ((), (), s32[]{:S(2)}) async-start(), calls=%async_computation.16 | async-start | bytes 6553600 | tf_op jit(solution)/shard_map/reduce_scatter | solution.py:188
  1381.2 725.4 %reduce-scatter.18.cloned.1.call-start = ((), (), s32[]{:S(2)}) async-start(), calls=%async_computation.19 | async-start | bytes 3538944 | tf_op jit(solution)/shard_map/reduce_scatter | solution.py:319
  1486.9 14.9 copy-start.24
  1486.9 14.9 copy-start.26
  1486.9 14.9 copy-start.34
  1486.9 14.9 copy-start.40
  1486.9 14.9 copy-start.44
  1486.9 14.9 copy-start.48
  1486.9 14.9 copy-start.54
  1486.9 27.5 %slice-start.3 = ((s8[5242880]{0:T(1024)(128)(4,1)}), s8[1048576]{0:T(1024)(128)(4,1)S(1)}, s32[]{:S(2)}) async-start(s8[5242880]{0:T(1024)(128)(4,1)} %bitcast.214), calls=%async_computation.29 | async-start | bytes 2097152
  1526.0 425.7 %copy-start.36 = (f32[2560]{0:T(1024)S(1)}, f32[2560]{0:T(1024)}, u32[]{:S(2)}) copy-start(f32[2560]{0:T(1024)} %copy-done.35) | copy-start | bytes 30724
  1526.0 425.7 %copy-start.42 = (f32[2560]{0:T(1024)S(1)}, f32[2560]{0:T(1024)}, u32[]{:S(2)}) copy-start(f32[2560]{0:T(1024)} %copy-done.41) | copy-start | bytes 30724
  1526.0 425.7 %copy-start.56 = (f32[1024]{0:T(1024)S(1)}, f32[1024]{0:T(1024)}, u32[]{:S(2)}) copy-start(f32[1024]{0:T(1024)} %param.22) | copy-start | bytes 12292
  1593.8 13.5 copy-start.6
  1593.8 13.5 copy-start.8
  1677.4 13.4 copy-start.8
  1760.9 13.4 copy-start.8
  1844.5 13.4 copy-start.8
  1928.1 13.4 copy-start.8
  1961.4 147.1 %reduce-scatter.16.cloned.1.call-start = ((), (), s32[]{:S(2)}) async-start(), calls=%async_computation.18 | async-start | bytes 6553600 | tf_op jit(solution)/shard_map/reduce_scatter | solution.py:311
  1973.4 175.1 %reduce-scatter.26.cloned.1.call-start = ((), (), s32[]{:S(2)}) async-start(), calls=%async_computation.23 | async-start | bytes 36864 | tf_op jit(solution)/shard_map/reduce_scatter | solution.py:324
  1977.4 263.1 %reduce-scatter.24.cloned.1.call-start = ((), (), s32[]{:S(2)}) async-start(), calls=%async_computation.22 | async-start | bytes 4718592 | tf_op jit(solution)/shard_map/reduce_scatter | solution.py:323
  1988.1 344.2 %reduce-scatter.22.cloned.1.call-start = ((), (), s32[]{:S(2)}) async-start(), calls=%async_computation.21 | async-start | bytes 4718592 | tf_op jit(solution)/shard_map/reduce_scatter | solution.py:322
  1998.8 401.5 %reduce-scatter.20.cloned.1.call-start = ((), (), s32[]{:S(2)}) async-start(), calls=%async_computation.20 | async-start | bytes 1179648 | tf_op jit(solution)/shard_map/reduce_scatter | solution.py:320
  2001.7 17.8 slice-start
  2005.5 14.0 slice-start.1
  2005.5 14.0 slice-start.2
  2005.5 14.0 copy-start.13
  2022.1 13.5 copy-start.57
  2057.8 342.4 %copy-start.1 = (bf16[1,1024,1024]{2,1,0:T(8,128)(2,1)S(1)}, bf16[1,1024,1024]{2,1,0:T(8,128)(2,1)}, u32[]{:S(2)}) copy-start(bf16[1,1024,1024]{2,1,0:T(8,128)(2,1)} %param.30) | copy-start | bytes 6291460
  (54 other events, 308.9 us)
Sparse Core Ops, SparseCore 0:
  9.6 43.1 all-gather.5
  272.2 85.2 reduce-scatter.11
  361.6 70.1 all-gather.7
  686.4 40.8 all-gather.9
  1356.7 130.1 all-gather.11
  1490.1 61.8 reduce-scatter.27
  1554.7 50.5 reduce-scatter.13
  1961.5 75.7 reduce-scatter.17
  2039.9 51.2 reduce-scatter.15
  2095.0 53.4 reduce-scatter.25
  2153.1 87.3 reduce-scatter.23
  2244.6 87.6 reduce-scatter.21
  2336.6 63.5 reduce-scatter.19
